TPU v7x, 256 devices: a whole 4x4x8 slice. The times are simulated.
256 devices in a mesh: sub: 256 (over z, y, x, core).
Axes of the slice: x: 4, y: 4, z: 8, core: 2. Of those that a mesh axis runs over, the one named last changes fastest.
Arguments:
- stiffness: float32 [256, 1024, 1024], P('sub'), as said below
- neumann_inv: float32 [256, 1024, 1024], P('sub'), as said below
- coarse_basis: float32 [256, 16, 1024], P('sub'), may hold values from -0.375 to 0.375
- coarse_inv: float32 [4096, 4096], P('sub'), as said below
- loads: float32 [256, 64, 1024], P('sub'), may hold values from -6 to 6
- face_index: int32 [256, 4, 128], P('sub'), may hold values from 0 to 1023, as said below
- face_len: int32 [256, 4], P('sub'), may hold values from 0 to 128, as said below
Outputs:
- solution: float32 [256, 64, 1024], P('sub')
- residual: float32 [256, 64, 1024], P('sub')
Inputs may be any that keep to these rules, and one draw needn't show every extreme that they name: `face_index`: within one subdomain all 512 entries are distinct. `face_len`: A block without a neighbour has length 0; paired blocks of two neighbours have equal length; some block has length 128. `stiffness`: each matrix is exactly symmetric and positive definite. `neumann_inv`: each matrix is exactly symmetric and positive definite. `coarse_inv`: the matrix is exactly symmetric and positive definite.
All inputs are finite; a program needn't handle non-finite values.
Results may differ from a plain program's by a relative error of at most 0.00022.
Values sent between devices are 32-bit elements; how exact they have to be, the bound alone decides.
A program may use at most 64 MiB of HBM per device.

v0:
```python
import jax
import jax.numpy as jnp
from jax import lax
from jax.sharding import PartitionSpec as P

CYCLE = 16
ITERS = 4
HIGH = lax.Precision.HIGHEST


def from_behind(value, axis, by):
    length = lax.axis_size(axis)
    pairs = [(i, i + by) for i in range(length) if 0 <= i + by < length]
    return lax.ppermute(value, axis, pairs)


def local(stiffness, neumann_inv, coarse_basis, coarse_inv, loads, face_index, face_len):
    stiff = stiffness[0]
    local_inv = neumann_inv[0]
    basis = coarse_basis[0]
    width = face_index.shape[2]
    face_slots = face_index[0].reshape(-1)
    slot_pos = jnp.arange(width, dtype=jnp.int32)
    live_slots = (slot_pos[None, :] < face_len[0][:, None]).astype(jnp.float32).reshape(-1)
    counts = jnp.ones((stiff.shape[0],), jnp.float32).at[face_slots].add(live_slots)
    weight = 1.0 / counts

    def assemble(local_vals):
        cases = local_vals.shape[0]
        face_vals = jnp.take(local_vals, face_slots, axis=1) * live_slots[None, :]
        blocks = face_vals.reshape(cases, 4, width)
        west_in = from_behind(blocks[:, 1], "sub", 1)
        east_in = from_behind(blocks[:, 0], "sub", -1)
        south_in = from_behind(blocks[:, 3], "sub", CYCLE)
        north_in = from_behind(blocks[:, 2], "sub", -CYCLE)
        incoming = jnp.stack([west_in, east_in, south_in, north_in], axis=1).reshape(cases, -1)
        incoming = incoming * live_slots[None, :]
        return local_vals.at[:, face_slots].add(incoming)

    def inner(left, right):
        return jnp.sum(left * right * weight[None, :], axis=1)

    def coarse_solve(coarse_res):
        return jnp.dot(
            coarse_inv, lax.all_gather(coarse_res, "sub", axis=0, tiled=True), precision=HIGH
        )

    def precond(resid):
        scaled = weight[None, :] * resid
        local_sol = jnp.dot(scaled, local_inv, precision=HIGH)
        coarse_res = jnp.einsum("cn,kn->ck", basis, scaled, precision=HIGH)
        coarse_sol = coarse_solve(coarse_res)
        local_sol = local_sol + jnp.einsum("ck,cn->kn", coarse_sol, basis, precision=HIGH)
        return assemble(weight[None, :] * local_sol)

    def progress_sum(resid, precond_res):
        return lax.psum(inner(resid, precond_res), "sub")

    residual = assemble(loads[0])
    solution = jnp.zeros_like(residual)
    precond_res = precond(residual)
    direction = precond_res
    rz_now = progress_sum(residual, precond_res)
    for step in range(ITERS):
        image = assemble(jnp.dot(direction, stiff, precision=HIGH))
        alpha = rz_now / lax.psum(inner(direction, image), "sub")
        solution = solution + alpha[:, None] * direction
        residual = residual - alpha[:, None] * image
        if step + 1 < ITERS:
            precond_res = precond(residual)
            rz_next = progress_sum(residual, precond_res)
            direction = precond_res + (rz_next / rz_now)[:, None] * direction
            rz_now = rz_next
    return (solution[None], residual[None])


def solution(mesh):
    placed = (
        P("sub", None, None),
        P("sub", None, None),
        P("sub", None, None),
        P("sub", None),
        P("sub", None, None),
        P("sub", None, None),
        P("sub", None),
    )
    return jax.shard_map(
        local,
        mesh=mesh,
        in_specs=placed,
        out_specs=(P("sub", None, None), P("sub", None, None)),
        check_vma=False,
    )
```

profile of v0, /device:TPU:1, one launch (start us, length us, event | category | flops | bytes accessed | tf_op | source)
XLA Modules:
  0.0 1297.2 jit_solution(2350251910647447329)
XLA Ops:
  17.6 5.5 collective-permute-start.2
  35.3 111.1 %all-gather.5.cloned.1.call-done = f32[4096,64]{1,0:T(8,128)} async-done(((f32[16,64]{1,0:T(8,128)}), f32[4096,64]{1,0:T(8,128)}) %all-gather.5.cloned.1.call-update) | async-done | bytes 1048592 | tf_op jit(solution)/shard_map/all_gather | solution.py:45
  146.4 5.0 fusion.88
  151.8 4.8 fusion.19
  162.7 5.5 collective-permute-start.6
  177.9 8.5 fusion.6
  190.9 6.0 collective-permute-start.10
  206.8 90.3 %all-reduce = (f32[64]{0:T(128)S(1)}, f32[64]{0:T(128)S(1)}) all-reduce(f32[64]{0:T(128)S(1)} %get-tuple-element.4, f32[64]{0:T(128)S(1)} %get-tuple-element.3), channel_id=1, replica_groups=mesh['sub'=256] {'sub'}, use_global_device_ids=true, to_apply=%region_4.6 | all-reduce | flops 128 | bytes 1024 | tf_op jit(solution)/shard_map/psum | solution.py:57
  298.4 100.4 %all-gather.7.cloned.1.call-done = f32[4096,64]{1,0:T(8,128)} async-done(((f32[16,64]{1,0:T(8,128)}), f32[4096,64]{1,0:T(8,128)}) %all-gather.7.cloned.1.call-update) | async-done | bytes 1048592 | tf_op jit(solution)/shard_map/all_gather | solution.py:45
  398.8 5.0 fusion.89
  404.1 4.8 fusion.25
  415.0 5.5 collective-permute-start.14
  430.1 83.8 %psum.58 = f32[64]{0:T(128)S(1)} all-reduce(f32[64]{0:T(128)S(1)} %multiply_reduce_fusion.5), channel_id=1, replica_groups=mesh['sub'=256] {'sub'}, use_global_device_ids=true, to_apply=%region_10.12 | all-reduce | flops 64 | bytes 512 | tf_op jit(solution)/shard_map/psum | solution.py:57
  514.0 8.5 fusion.4
  527.0 5.5 collective-permute-start.18
  542.1 85.6 %psum.59 = f32[64]{0:T(128)S(1)} all-reduce(f32[64]{0:T(128)S(1)} %multiply_reduce_fusion.4), channel_id=1, replica_groups=mesh['sub'=256] {'sub'}, use_global_device_ids=true, to_apply=%region_13.15 | all-reduce | flops 64 | bytes 512 | tf_op jit(solution)/shard_map/psum | solution.py:66
  629.1 100.3 %all-gather.9.cloned.1.call-done = f32[4096,64]{1,0:T(8,128)} async-done(((f32[16,64]{1,0:T(8,128)}), f32[4096,64]{1,0:T(8,128)}) %all-gather.9.cloned.1.call-update) | async-done | bytes 1048592 | tf_op jit(solution)/shard_map/all_gather | solution.py:45
  729.4 5.0 fusion.90
  734.8 4.8 fusion.31
  745.7 5.5 collective-permute-start.22
  760.8 84.0 %psum.60 = f32[64]{0:T(128)S(1)} all-reduce(f32[64]{0:T(128)S(1)} %multiply_reduce_fusion.3), channel_id=1, replica_groups=mesh['sub'=256] {'sub'}, use_global_device_ids=true, to_apply=%region_16.18 | all-reduce | flops 64 | bytes 512 | tf_op jit(solution)/shard_map/psum | solution.py:57
  844.9 8.5 fusion.2
  857.9 5.5 collective-permute-start.26
  873.0 85.8 %psum.61 = f32[64]{0:T(128)S(1)} all-reduce(f32[64]{0:T(128)S(1)} %multiply_reduce_fusion.2), channel_id=1, replica_groups=mesh['sub'=256] {'sub'}, use_global_device_ids=true, to_apply=%region_19.21 | all-reduce | flops 64 | bytes 512 | tf_op jit(solution)/shard_map/psum | solution.py:66
  959.8 100.6 %all-gather.11.cloned.1.call-done = f32[4096,64]{1,0:T(8,128)} async-done(((f32[16,64]{1,0:T(8,128)}), f32[4096,64]{1,0:T(8,128)}) %all-gather.11.cloned.1.call-update) | async-done | bytes 1048592 | tf_op jit(solution)/shard_map/all_gather | solution.py:45
  1060.5 5.0 fusion.91
  1065.8 4.8 fusion.37
  1076.7 5.5 collective-permute-start.30
  1091.8 83.8 %psum.62 = f32[64]{0:T(128)S(1)} all-reduce(f32[64]{0:T(128)S(1)} %multiply_reduce_fusion.1), channel_id=1, replica_groups=mesh['sub'=256] {'sub'}, use_global_device_ids=true, to_apply=%region_22.24 | all-reduce | flops 64 | bytes 512 | tf_op jit(solution)/shard_map/psum | solution.py:57
  1175.6 8.5 fusion
  1188.6 5.5 collective-permute-start.34
  1203.8 85.6 %psum.63 = f32[64]{0:T(128)S(1)} all-reduce(f32[64]{0:T(128)S(1)} %multiply_reduce_fusion), channel_id=1, replica_groups=mesh['sub'=256] {'sub'}, use_global_device_ids=true, to_apply=%region_25.27 | all-reduce | flops 64 | bytes 512 | tf_op jit(solution)/shard_map/psum | solution.py:66
  (178 shorter events, 147.3 us)
Async XLA Ops:
  7.2 139.2 %all-gather.5.cloned.1.call-start = ((), (), s32[]{:S(2)}) async-start(), calls=%async_computation | async-start | bytes 2105344 | tf_op jit(solution)/shard_map/all_gather | solution.py:45
  11.8 18.6 %collective-permute-start = (f32[64,128]{0,1:T(8,128)S(1)}, f32[64,128]{0,1:T(8,128)S(1)}, u32[]{:S(2)}, u32[]{:S(2)}) collective-permute-start(f32[64,128]{0,1:T(8,128)S(1)} %get-tuple-element.39), channel_id=1, source_target_pairs={{0,1},{1,2},{2,3},{3,4},{4,5},{5,6},{6,7},{7,8},{8,9},{9,10},{10,1... | collective-permute-start | bytes 98312 | tf_op jit(solution)/shard_map/ppermute | solution.py:14
  16.3 14.1 %collective-permute-start.3 = (f32[64,128]{0,1:T(8,128)S(1)}, f32[64,128]{0,1:T(8,128)S(1)}, u32[]{:S(2)}, u32[]{:S(2)}) collective-permute-start(f32[64,128]{0,1:T(8,128)S(1)} %get-tuple-element.40), channel_id=1, source_target_pairs={{16,0},{17,1},{18,2},{19,3},{20,4},{21,5},{22,6},{23,7},{24,8},{25... | collective-permute-start | bytes 98312 | tf_op jit(solution)/shard_map/ppermute | solution.py:14
  17.6 12.8 collective-permute-start.2
  23.1 7.3 collective-permute-start.1
  35.3 363.5 %all-gather.7.cloned.1.call-start = ((), (), s32[]{:S(2)}) async-start(), calls=%async_computation.1 | async-start | bytes 2105344 | tf_op jit(solution)/shard_map/all_gather | solution.py:45
  158.1 12.0 collective-permute-start.4
  161.4 8.7 collective-permute-start.7
  162.7 7.5 collective-permute-start.6
  187.7 12.2 collective-permute-start.8
  189.6 10.3 collective-permute-start.11
  190.9 9.0 collective-permute-start.10
  298.2 431.2 %all-gather.9.cloned.1.call-start = ((), (), s32[]{:S(2)}) async-start(), calls=%async_computation.2 | async-start | bytes 2105344 | tf_op jit(solution)/shard_map/all_gather | solution.py:45
  410.5 12.0 collective-permute-start.12
  413.7 8.7 collective-permute-start.15
  415.0 7.5 collective-permute-start.14
  523.8 11.7 collective-permute-start.16
  525.7 9.8 collective-permute-start.19
  527.0 8.5 collective-permute-start.18
  628.8 431.6 %all-gather.11.cloned.1.call-start = ((), (), s32[]{:S(2)}) async-start(), calls=%async_computation.3 | async-start | bytes 2105344 | tf_op jit(solution)/shard_map/all_gather | solution.py:45
  741.1 12.0 collective-permute-start.20
  744.4 8.7 collective-permute-start.23
  745.7 7.5 collective-permute-start.22
  854.7 11.7 collective-permute-start.24
  856.6 9.8 collective-permute-start.27
  857.9 8.5 collective-permute-start.26
  1072.1 12.0 collective-permute-start.28
  1075.4 8.7 collective-permute-start.31
  1076.7 7.5 collective-permute-start.30
  1185.4 11.7 collective-permute-start.32
  1187.3 9.8 collective-permute-start.35
  1188.6 8.5 collective-permute-start.34
  (10 other events, 211.3 us)
Sparse Core Ops, SparseCore 0:
  35.4 110.9 all-gather.4
  298.3 100.4 all-gather.6
  628.9 100.4 all-gather.8
  960.0 100.4 all-gather.10
where the time goes:
time: 1310 us; the launch traced here: 1300 us
  blocking collectives  599 us (46%)
  waiting for transfers between devices  438 us (33%)
  starting transfers between devices  109 us (8%)
  matrix products  78.4 us (6%)
  other arithmetic  44.7 us (3%)
  between operations  15.2 us (1%)
  local copies, waits for them, and re-layouts  13.1 us (1%)
    all_gather x4, waiting for transfers between devices, coarse_solve(): lax.all_gather(coarse_res, 'sub', axis=0, tiled=True)  412 us
    psum x4, blocking collectives, progress_sum(): return lax.psum(inner(resid, precond_res), 'sub')  342 us
    psum x3, blocking collectives, local(): alpha = rz_now / lax.psum(inner(direction, image), 'sub')  257 us
    ppermute x36, starting transfers between devices, from_behind(): return lax.ppermute(value, axis, pairs)  109 us
    dot_general x4, matrix products, local(): image = assemble(jnp.dot(direction, stiff, precision=HIGH))  34 us
    scatter-add x9, other arithmetic, assemble(): return local_vals.at[:, face_slots].add(incoming)  32.2 us
  transfers between devices with their start and end apart: 40, of which 12 were waited for; matrix products, arithmetic and copies ran while one was open for 0% of the time, Pallas kernels for 0%

commit v1 on v0

--- a/solution.py
+++ b/solution.py
@@ -42,7 +42,11 @@
 
     def coarse_solve(coarse_res):
         return jnp.dot(
-            coarse_inv, lax.all_gather(coarse_res, "sub", axis=0, tiled=True), precision=HIGH
+            coarse_inv,
+            jnp.concatenate(
+                lax.all_to_all(jnp.stack([coarse_res] * lax.axis_size("sub")), "sub", 0, 0), axis=0
+            ),
+            precision=HIGH,
         )
 
     def precond(resid):

time: 1310 us -> 1070 us (0.82)
  waiting for transfers between devices: 438 us -> 24.5 us
  blocking collectives: 599 us -> 762 us
  other arithmetic: 44.7 us -> 62.1 us
  local copies, waits for them, and re-layouts: 13.1 us -> 30.2 us
    all_gather x4 -> x0, waiting for transfers between devices: 412 us -> none  [coarse_solve(): lax.all_gather(coarse_res, 'sub', axis=0, tiled=True)]
    all_to_all x0 -> x4, blocking collectives: none -> 165 us  [coarse_solve(): lax.all_to_all(jnp.stack([coarse_res] * lax.axis_size('sub')), 'sub', 0, 0)]
    all_to_all x0 -> x4, other arithmetic: none -> 17.4 us  [coarse_solve(): lax.all_to_all(jnp.stack([coarse_res] * lax.axis_size('sub')), 'sub', 0, 0)]
    unnamed x5 -> x17, local copies, waits for them, and re-layouts: 1.16 us -> 17.1 us
  transfers between devices with their start and end apart: 40 -> 36, of which waited for: 12 -> 8; matrix products, arithmetic and copies ran while one was open for 0% -> 0% of each run, Pallas kernels for 0% -> 0%
where the time goes in v1:
time: 1070 us; the launch traced here: 1060 us
  blocking collectives  762 us (71%)
  starting transfers between devices  110 us (10%)
  matrix products  69.5 us (6%)
  other arithmetic  62.1 us (6%)
  local copies, waits for them, and re-layouts  30.2 us (3%)
  waiting for transfers between devices  24.5 us (2%)
    psum x4, blocking collectives, progress_sum(): return lax.psum(inner(resid, precond_res), 'sub')  340 us
    psum x3, blocking collectives, local(): alpha = rz_now / lax.psum(inner(direction, image), 'sub')  257 us
    all_to_all x4, blocking collectives, coarse_solve(): lax.all_to_all(jnp.stack([coarse_res] * lax.axis_size('sub')), 'sub', 0, 0)  165 us
    ppermute x36, starting transfers between devices, from_behind(): return lax.ppermute(value, axis, pairs)  110 us
    dot_general x4, matrix products, local(): image = assemble(jnp.dot(direction, stiff, precision=HIGH))  34 us
    scatter-add x9, other arithmetic, assemble(): return local_vals.at[:, face_slots].add(incoming)  32.1 us
    ppermute x36, waiting for transfers between devices, from_behind(): return lax.ppermute(value, axis, pairs)  24.5 us
  transfers between devices with their start and end apart: 36, of which 8 were waited for; matrix products, arithmetic and copies ran while one was open for 0% of the time, Pallas kernels for 0%

profile of v1, /device:TPU:1, one launch (start us, length us, event | category | flops | bytes accessed | tf_op | source)
XLA Modules:
  0.0 1060.0 jit_solution(10309809624951423216)
XLA Ops:
  5.2 4.5 collective-permute-start
  11.1 5.5 collective-permute-start.2
  30.5 49.1 %all_to_all.20 = f32[256,1,1024]{2,1,0:T(1,128)S(1)} all-to-all(f32[256,1,1024]{2,1,0:T(1,128)} %reshape.362), channel_id=1, replica_groups=mesh['sub'=256] {'sub'}, dimensions={0} | all-to-all | bytes 2097152 | tf_op jit(solution)/shard_map/all_to_all | solution.py:47
  89.9 4.8 fusion.19
  101.0 5.5 collective-permute-start.6
  116.2 8.5 fusion.6
  129.2 5.8 collective-permute-start.10
  144.6 90.2 %all-reduce = (f32[64]{0:T(128)S(1)}, f32[64]{0:T(128)S(1)}) all-reduce(f32[64]{0:T(128)S(1)} %get-tuple-element.4, f32[64]{0:T(128)S(1)} %get-tuple-element.3), channel_id=1, replica_groups=mesh['sub'=256] {'sub'}, use_global_device_ids=true, to_apply=%region_4.6 | all-reduce | flops 128 | bytes 1024 | tf_op jit(solution)/shard_map/psum | solution.py:61
  237.7 38.5 %all_to_all.21 = f32[256,1,1024]{2,1,0:T(1,128)S(1)} all-to-all(f32[256,1,1024]{2,1,0:T(1,128)} %reshape.364), channel_id=1, replica_groups=mesh['sub'=256] {'sub'}, dimensions={0} | all-to-all | bytes 2097152 | tf_op jit(solution)/shard_map/all_to_all | solution.py:47
  276.3 4.4 reduce.1
  286.1 4.8 fusion.25
  297.2 5.5 collective-permute-start.14
  312.3 83.3 %psum.58 = f32[64]{0:T(128)S(1)} all-reduce(f32[64]{0:T(128)S(1)} %multiply_reduce_fusion.5), channel_id=1, replica_groups=mesh['sub'=256] {'sub'}, use_global_device_ids=true, to_apply=%region_10.12 | all-reduce | flops 64 | bytes 512 | tf_op jit(solution)/shard_map/psum | solution.py:61
  395.7 8.5 fusion.4
  408.7 5.5 collective-permute-start.18
  423.7 85.6 %psum.59 = f32[64]{0:T(128)S(1)} all-reduce(f32[64]{0:T(128)S(1)} %multiply_reduce_fusion.4), channel_id=1, replica_groups=mesh['sub'=256] {'sub'}, use_global_device_ids=true, to_apply=%region_13.15 | all-reduce | flops 64 | bytes 512 | tf_op jit(solution)/shard_map/psum | solution.py:70
  512.2 38.8 %all_to_all.22 = f32[256,1,1024]{2,1,0:T(1,128)S(1)} all-to-all(f32[256,1,1024]{2,1,0:T(1,128)} %reshape.366), channel_id=1, replica_groups=mesh['sub'=256] {'sub'}, dimensions={0} | all-to-all | bytes 2097152 | tf_op jit(solution)/shard_map/all_to_all | solution.py:47
  551.0 4.4 reduce.2
  560.8 4.8 fusion.31
  571.9 5.5 collective-permute-start.22
  587.0 83.2 %psum.60 = f32[64]{0:T(128)S(1)} all-reduce(f32[64]{0:T(128)S(1)} %multiply_reduce_fusion.3), channel_id=1, replica_groups=mesh['sub'=256] {'sub'}, use_global_device_ids=true, to_apply=%region_16.18 | all-reduce | flops 64 | bytes 512 | tf_op jit(solution)/shard_map/psum | solution.py:61
  670.3 8.5 fusion.2
  683.3 5.5 collective-permute-start.26
  698.4 85.6 %psum.61 = f32[64]{0:T(128)S(1)} all-reduce(f32[64]{0:T(128)S(1)} %multiply_reduce_fusion.2), channel_id=1, replica_groups=mesh['sub'=256] {'sub'}, use_global_device_ids=true, to_apply=%region_19.21 | all-reduce | flops 64 | bytes 512 | tf_op jit(solution)/shard_map/psum | solution.py:70
  786.9 38.6 %all_to_all.23 = f32[256,1,1024]{2,1,0:T(1,128)S(1)} all-to-all(f32[256,1,1024]{2,1,0:T(1,128)} %reshape.368), channel_id=1, replica_groups=mesh['sub'=256] {'sub'}, dimensions={0} | all-to-all | bytes 2097152 | tf_op jit(solution)/shard_map/all_to_all | solution.py:47
  825.4 4.4 reduce.3
  835.3 4.8 fusion.37
  846.4 5.5 collective-permute-start.30
  861.4 83.3 %psum.62 = f32[64]{0:T(128)S(1)} all-reduce(f32[64]{0:T(128)S(1)} %multiply_reduce_fusion.1), channel_id=1, replica_groups=mesh['sub'=256] {'sub'}, use_global_device_ids=true, to_apply=%region_22.24 | all-reduce | flops 64 | bytes 512 | tf_op jit(solution)/shard_map/psum | solution.py:61
  944.8 8.6 fusion
  957.9 5.5 collective-permute-start.34
  973.0 85.6 %psum.63 = f32[64]{0:T(128)S(1)} all-reduce(f32[64]{0:T(128)S(1)} %multiply_reduce_fusion), channel_id=1, replica_groups=mesh['sub'=256] {'sub'}, use_global_device_ids=true, to_apply=%region_25.27 | all-reduce | flops 64 | bytes 512 | tf_op jit(solution)/shard_map/psum | solution.py:70
  (191 shorter events, 175.4 us)
Async XLA Ops:
  5.2 18.6 %collective-permute-start = (f32[64,128]{0,1:T(8,128)S(1)}, f32[64,128]{0,1:T(8,128)S(1)}, u32[]{:S(2)}, u32[]{:S(2)}) collective-permute-start(f32[64,128]{0,1:T(8,128)S(1)} %get-tuple-element.39), channel_id=1, source_target_pairs={{0,1},{1,2},{2,3},{3,4},{4,5},{5,6},{6,7},{7,8},{8,9},{9,10},{10,1... | collective-permute-start | bytes 98312 | tf_op jit(solution)/shard_map/ppermute | solution.py:14
  9.8 14.1 %collective-permute-start.3 = (f32[64,128]{0,1:T(8,128)S(1)}, f32[64,128]{0,1:T(8,128)S(1)}, u32[]{:S(2)}, u32[]{:S(2)}) collective-permute-start(f32[64,128]{0,1:T(8,128)S(1)} %get-tuple-element.40), channel_id=1, source_target_pairs={{16,0},{17,1},{18,2},{19,3},{20,4},{21,5},{22,6},{23,7},{24,8},{25... | collective-permute-start | bytes 98312 | tf_op jit(solution)/shard_map/ppermute | solution.py:14
  11.1 12.8 %collective-permute-start.2 = (f32[64,128]{0,1:T(8,128)S(1)}, f32[64,128]{0,1:T(8,128)S(1)}, u32[]{:S(2)}, u32[]{:S(2)}) collective-permute-start(f32[64,128]{0,1:T(8,128)S(1)} %get-tuple-element.41), channel_id=1, source_target_pairs={{0,16},{1,17},{2,18},{3,19},{4,20},{5,21},{6,22},{7,23},{8,24},{9,... | collective-permute-start | bytes 98312 | tf_op jit(solution)/shard_map/ppermute | solution.py:14
  16.6 7.3 collective-permute-start.1
  96.3 12.2 %collective-permute-start.4 = (f32[64,128]{0,1:T(8,128)S(1)}, f32[64,128]{0,1:T(8,128)S(1)}, u32[]{:S(2)}, u32[]{:S(2)}) collective-permute-start(f32[64,128]{0,1:T(8,128)S(1)} %get-tuple-element.35), channel_id=1, source_target_pairs={{0,1},{1,2},{2,3},{3,4},{4,5},{5,6},{6,7},{7,8},{8,9},{9,10},{10,1... | collective-permute-start | bytes 98312 | tf_op jit(solution)/shard_map/ppermute | solution.py:14
  99.7 8.7 collective-permute-start.7
  101.0 7.5 collective-permute-start.6
  106.5 5.6 collective-permute-start.5
  126.0 12.4 %collective-permute-start.8 = (f32[64,128]{0,1:T(8,128)S(1)}, f32[64,128]{0,1:T(8,128)S(1)}, u32[]{:S(2)}, u32[]{:S(2)}) collective-permute-start(f32[64,128]{0,1:T(8,128)S(1)} %get-tuple-element.31), channel_id=1, source_target_pairs={{0,1},{1,2},{2,3},{3,4},{4,5},{5,6},{6,7},{7,8},{8,9},{9,10},{10,1... | collective-permute-start | bytes 98312 | tf_op jit(solution)/shard_map/ppermute | solution.py:14
  127.9 10.5 collective-permute-start.11
  129.2 9.2 collective-permute-start.10
  135.0 5.6 collective-permute-start.9
  292.4 12.2 %collective-permute-start.12 = (f32[64,128]{0,1:T(8,128)S(1)}, f32[64,128]{0,1:T(8,128)S(1)}, u32[]{:S(2)}, u32[]{:S(2)}) collective-permute-start(f32[64,128]{0,1:T(8,128)S(1)} %get-tuple-element.27), channel_id=1, source_target_pairs={{0,1},{1,2},{2,3},{3,4},{4,5},{5,6},{6,7},{7,8},{8,9},{9,10},{10,1... | collective-permute-start | bytes 98312 | tf_op jit(solution)/shard_map/ppermute | solution.py:14
  295.9 8.7 collective-permute-start.15
  297.2 7.5 collective-permute-start.14
  302.7 5.6 collective-permute-start.13
  405.4 11.7 %collective-permute-start.16 = (f32[64,128]{0,1:T(8,128)S(1)}, f32[64,128]{0,1:T(8,128)S(1)}, u32[]{:S(2)}, u32[]{:S(2)}) collective-permute-start(f32[64,128]{0,1:T(8,128)S(1)} %get-tuple-element.23), channel_id=1, source_target_pairs={{0,1},{1,2},{2,3},{3,4},{4,5},{5,6},{6,7},{7,8},{8,9},{9,10},{10,1... | collective-permute-start | bytes 98312 | tf_op jit(solution)/shard_map/ppermute | solution.py:14
  407.4 9.8 collective-permute-start.19
  408.7 8.5 collective-permute-start.18
  414.2 5.6 collective-permute-start.17
  567.1 12.2 %collective-permute-start.20 = (f32[64,128]{0,1:T(8,128)S(1)}, f32[64,128]{0,1:T(8,128)S(1)}, u32[]{:S(2)}, u32[]{:S(2)}) collective-permute-start(f32[64,128]{0,1:T(8,128)S(1)} %get-tuple-element.19), channel_id=1, source_target_pairs={{0,1},{1,2},{2,3},{3,4},{4,5},{5,6},{6,7},{7,8},{8,9},{9,10},{10,1... | collective-permute-start | bytes 98312 | tf_op jit(solution)/shard_map/ppermute | solution.py:14
  570.6 8.7 collective-permute-start.23
  571.9 7.5 collective-permute-start.22
  680.1 11.7 %collective-permute-start.24 = (f32[64,128]{0,1:T(8,128)S(1)}, f32[64,128]{0,1:T(8,128)S(1)}, u32[]{:S(2)}, u32[]{:S(2)}) collective-permute-start(f32[64,128]{0,1:T(8,128)S(1)} %get-tuple-element.15), channel_id=1, source_target_pairs={{0,1},{1,2},{2,3},{3,4},{4,5},{5,6},{6,7},{7,8},{8,9},{9,10},{10,1... | collective-permute-start | bytes 98312 | tf_op jit(solution)/shard_map/ppermute | solution.py:14
  682.0 9.8 collective-permute-start.27
  683.3 8.5 collective-permute-start.26
  841.6 12.2 %collective-permute-start.28 = (f32[64,128]{0,1:T(8,128)S(1)}, f32[64,128]{0,1:T(8,128)S(1)}, u32[]{:S(2)}, u32[]{:S(2)}) collective-permute-start(f32[64,128]{0,1:T(8,128)S(1)} %get-tuple-element.11), channel_id=1, source_target_pairs={{0,1},{1,2},{2,3},{3,4},{4,5},{5,6},{6,7},{7,8},{8,9},{9,10},{10,1... | collective-permute-start | bytes 98312 | tf_op jit(solution)/shard_map/ppermute | solution.py:14
  845.1 8.7 collective-permute-start.31
  846.4 7.5 collective-permute-start.30
  954.6 11.7 %collective-permute-start.32 = (f32[64,128]{0,1:T(8,128)S(1)}, f32[64,128]{0,1:T(8,128)S(1)}, u32[]{:S(2)}, u32[]{:S(2)}) collective-permute-start(f32[64,128]{0,1:T(8,128)S(1)} %get-tuple-element.7), channel_id=1, source_target_pairs={{0,1},{1,2},{2,3},{3,4},{4,5},{5,6},{6,7},{7,8},{8,9},{9,10},{10,1... | collective-permute-start | bytes 98312 | tf_op jit(solution)/shard_map/ppermute | solution.py:14
  956.6 9.8 collective-permute-start.35
  957.9 8.5 collective-permute-start.34
  (8 other events, 506.0 us)
